TPU v7x, 128 devices: a whole 4x4x4 slice. The times are simulated.
128 devices in a mesh: col: 32 (over z, y_hi, x), row: 4 (over y_lo, core).
Axes of the slice: x: 4, y: 4 (y_hi: 2, y_lo: 2; y = y_hi * 2 + y_lo), z: 4, core: 2. Of those that a mesh axis runs over, the one named last changes fastest.
Arguments:
- diffs: float32 [32768, 8192], P(('col', 'row')), as said below
- pairing: int32 [64], replicated, may hold values from 0 to 63, each once
Outputs:
- rotated: float32 [32, 4, 256, 8192], P(None, 'row', None, 'col')
Inputs may be any that keep to these rules, and one draw needn't show every extreme that they name: `pairing`: a permutation: every block index appears once. `diffs`: token rows with finite entries.
All inputs are finite; a program needn't handle non-finite values.
Results may differ from a plain program's by a relative error of at most 0.00025.
Values sent between devices are 32-bit elements; how exact they have to be, the bound alone decides.
No kernel may reach another device: no remote copies, remote signals or barrier semaphores. Data moves between devices by JAX's collectives and lax.ppermute only.
A program may use at most 128 MiB of HBM per device.

v0:
```python
import jax
import jax.numpy as jnp
from jax import lax
from jax.sharding import PartitionSpec as P

BLOCK = 128
JACOBI_STEPS = 2
INNER_STEPS = 2


def shifted(value, axis, steps):
    count = lax.axis_size(axis)
    leading, last = (max(0, -steps), min(count, count - steps))
    return lax.ppermute(value, axis, [(source, source + steps) for source in range(leading, last)])


def pair_rotation(pair_gram):
    rotation = jnp.eye(pair_gram.shape[0], dtype=jnp.float32)
    for repeat_index in range(INNER_STEPS):
        product = jnp.dot(
            pair_gram, rotation, precision=lax.Precision.HIGHEST, preferred_element_type=jnp.float32
        )
        normal_matrix = lax.dot_general(
            product,
            product,
            (((0,), (0,)), ((), ())),
            precision=lax.Precision.HIGHEST,
            preferred_element_type=jnp.float32,
        )
        factor = jnp.linalg.cholesky(normal_matrix)
        rotation = lax.linalg.triangular_solve(factor, product.T, left_side=True, lower=True).T
    return rotation


def local_gram(pair_rows):
    return lax.dot_general(
        pair_rows,
        pair_rows,
        (((0,), (0,)), ((), ())),
        precision=lax.Precision.HIGHEST,
        preferred_element_type=jnp.float32,
    )


def row_total(partial_gram):
    return lax.psum(partial_gram, "row")


def send_down(lower_half):
    return shifted(lower_half, "col", -1)


def send_up(outgoing):
    return shifted(outgoing, "col", 1)


def turn_and_move(pair_rows, rotation, position, col_count):
    turned = jnp.dot(
        pair_rows, rotation, precision=lax.Precision.HIGHEST, preferred_element_type=jnp.float32
    )
    upper_half = turned[:, :BLOCK]
    lower_half = turned[:, BLOCK:]
    from_above = send_down(lower_half)
    from_below = send_up(jnp.where(position == 0, lower_half, upper_half))
    new_upper = jnp.where(position == 0, upper_half, from_below)
    new_lower = jnp.where(position == col_count - 1, upper_half, from_above)
    return jnp.concatenate([new_upper, new_lower], axis=1)


def local(diffs, pairing):
    col_count = lax.axis_size("col")
    position = lax.axis_index("col")
    pair_width = 2 * BLOCK
    local_rows = diffs.shape[0]
    blocks = diffs.reshape(local_rows, 2 * col_count, BLOCK)
    ordered = jnp.take(blocks, pairing, axis=1).reshape(local_rows, col_count, pair_width)
    pair_rows = lax.all_to_all(ordered, "col", split_axis=1, concat_axis=0, tiled=True).reshape(
        -1, pair_width
    )
    pair_gram = row_total(local_gram(pair_rows))
    for jacobi_step in range(JACOBI_STEPS):
        if jacobi_step > 0:
            pair_gram = row_total(local_gram(pair_rows))
        rotation = pair_rotation(pair_gram)
        if jacobi_step + 1 < JACOBI_STEPS:
            pair_rows = turn_and_move(pair_rows, rotation, position, col_count)
        else:
            pair_rows = jnp.dot(
                pair_rows,
                rotation,
                precision=lax.Precision.HIGHEST,
                preferred_element_type=jnp.float32,
            )
    return pair_rows.reshape(col_count, 1, local_rows, pair_width)


def solution(mesh):
    in_specs = (P(("col", "row"), None), P())
    out_specs = P(None, "row", None, "col")
    return jax.shard_map(local, mesh=mesh, in_specs=in_specs, out_specs=out_specs, check_vma=False)
```

profile of v0, /device:TPU:1, one launch (start us, length us, event | category | flops | bytes accessed | tf_op | source)
XLA Modules:
  0.0 666.5 jit_solution(18403592186833088471)
XLA Ops:
  7.9 9.0 %copy.17 = f32[256,8192]{0,1:T(8,128)} copy(f32[256,8192]{1,0:T(8,128)} %param.5) | data formatting | bytes 16777216 | tf_op args[0]
  16.8 9.0 %copy.18 = f32[256,64,128]{2,0,1:T(8,128)} copy(f32[256,64,128]{0,2,1:T(8,128)} %bitcast.167) | data formatting | bytes 16777216 | tf_op jit(solution)/shard_map/reshape | solution.py:75
  25.8 7.9 %gather_fusion = f32[64,256,128]{2,1,0:T(8,128)} fusion(f32[256,64,128]{2,0,1:T(8,128)} %copy.18, s32[1024]{0:T(1024)S(1)} %pad_clamp_fusion), kind=kCustom, calls=%fused_computation | custom fusion | bytes 16777472 | tf_op jit(solution)/shard_map/jit(_take)/gather | solution.py:76
  33.7 9.0 %copy.19 = f32[256,64,128]{0,2,1:T(8,128)} copy(f32[256,64,128]{2,0,1:T(8,128)} %bitcast.165) | data formatting | bytes 16777216 | tf_op jit(solution)/shard_map/jit(_take)/gather | solution.py:76
  42.7 8.9 %copy.20 = f32[256,32,256]{2,0,1:T(8,128)} copy(f32[256,32,256]{0,2,1:T(8,128)} %bitcast.166) | data formatting | bytes 16777216 | tf_op jit(solution)/shard_map/jit(_take)/gather | solution.py:76
  51.9 4.3 broadcast_select_fusion
  56.2 106.7 %all_to_all.15 = f32[256,32,256]{2,0,1:T(8,128)S(1)} all-to-all(f32[256,32,256]{2,0,1:T(8,128)S(1)} %broadcast_select_fusion), channel_id=1, replica_groups=mesh['col'=32,'row'=4] {'col'}, dimensions={1} | all-to-all | bytes 16777216 | tf_op jit(solution)/shard_map/all_to_all | solution.py:77
  162.9 3.4 copy-done
  166.3 14.9 %fusion.4 = f32[256,256]{1,0:T(8,128)} fusion(f32[256,32,256]{2,0,1:T(8,128)S(1)} %all_to_all.15), kind=kOutput, calls=%fused_computation.18 | convolution fusion | flops 6442450944 | bytes 8650752 | tf_op jit(solution)/shard_map/dot_general | solution.py:36
  181.4 35.0 %all-reduce.4.cloned.1.call-done = f32[256,256]{1,0:T(8,128)} async-done(((f32[256,256]{1,0:T(8,128)}), f32[256,256]{1,0:T(8,128)}) %all-reduce.4.cloned.1.call-update) | async-done | bytes 262160 | tf_op jit(solution)/shard_map/psum | solution.py:46
  218.3 11.7 %cholesky.214 = f32[128,128]{1,0:T(8,128)S(1)} custom-call(f32[128,128]{1,0:T(8,128)S(1)} %cholesky.346), custom_call_target="Cholesky" | custom-call | tf_op jit(solution)/shard_map/jit(cholesky)/cholesky | solution.py:30
  230.1 9.8 %custom-call.17 = f32[1,128,128]{1,2,0:T(8,128)S(1)} custom-call(f32[1,128,128]{2,1,0:T(8,128)S(1)} %get-tuple-element.96), custom_call_target="InvertDiagBlocksLowerTriangular" | custom-call | tf_op jit(solution)/shard_map/jit(cholesky)/cholesky | solution.py:30
  240.4 11.7 %cholesky.231 = f32[128,128]{1,0:T(8,128)S(1)} custom-call(f32[128,128]{1,0:T(8,128)S(1)} %convolution_subtract_fusion.7), custom_call_target="Cholesky" | custom-call | tf_op jit(solution)/shard_map/jit(cholesky)/cholesky | solution.py:30
  254.2 4.2 while.8
  255.1 1.3 bitcast_dynamic-update-slice_fusion.8
  257.1 1.3 bitcast_dynamic-update-slice_fusion.8
  258.5 19.7 %custom-call.18 = f32[2,128,128]{1,2,0:T(8,128)S(1)} custom-call(f32[2,128,128]{2,1,0:T(8,128)S(1)} %get-tuple-element.33), custom_call_target="InvertDiagBlocksLowerTriangular" | custom-call | tf_op jit(solution)/shard_map/triangular_solve/custom-call.0 | solution.py:31
  279.2 1.4 fusion.7
  281.4 11.7 %cholesky.248 = f32[128,128]{1,0:T(8,128)S(1)} custom-call(f32[128,128]{1,0:T(8,128)S(1)} %cholesky.349), custom_call_target="Cholesky" | custom-call | tf_op jit(solution)/shard_map/jit(cholesky)/cholesky | solution.py:30
  293.1 9.8 %custom-call.19 = f32[1,128,128]{1,2,0:T(8,128)S(1)} custom-call(f32[1,128,128]{2,1,0:T(8,128)S(1)} %get-tuple-element.92), custom_call_target="InvertDiagBlocksLowerTriangular" | custom-call | tf_op jit(solution)/shard_map/jit(cholesky)/cholesky | solution.py:30
  303.4 11.7 %cholesky.265 = f32[128,128]{1,0:T(8,128)S(1)} custom-call(f32[128,128]{1,0:T(8,128)S(1)} %convolution_subtract_fusion.6), custom_call_target="Cholesky" | custom-call | tf_op jit(solution)/shard_map/jit(cholesky)/cholesky | solution.py:30
  317.8 4.3 while.9
  318.7 1.3 bitcast_dynamic-update-slice_fusion.9
  320.8 1.3 bitcast_dynamic-update-slice_fusion.9
  322.1 19.7 %custom-call.20 = f32[2,128,128]{1,2,0:T(8,128)S(1)} custom-call(f32[2,128,128]{2,1,0:T(8,128)S(1)} %get-tuple-element.34), custom_call_target="InvertDiagBlocksLowerTriangular" | custom-call | tf_op jit(solution)/shard_map/triangular_solve/custom-call.0 | solution.py:31
  342.8 10.7 %fusion.11 = f32[8192,256]{0,1:T(8,128)S(1)} fusion(f32[8192,256]{1,0:T(8,128)} %bitcast.164, f32[128,256]{1,0:T(8,128)S(1)} %fusion.45, f32[128,256]{1,0:T(8,128)S(1)} %fusion.32), kind=kOutput, calls=%fused_computation.35 | convolution fusion | flops 6442516480 | bytes 17039360 | tf_op jit(solution)/shard_map/dot_general | solution.py:58
  353.6 4.1 slice_select_fusion.2
  357.7 1.8 copy-done.1
  359.5 5.1 collective-permute-start
  364.5 1.7 collective-permute-start.1
  366.2 86.4 %collective-permute-done = f32[8192,128]{0,1:T(8,128)} collective-permute-done((f32[8192,128]{0,1:T(8,128)}, f32[8192,128]{0,1:T(8,128)}, u32[]{:S(2)}, u32[]{:S(2)}) %collective-permute-start) | collective-permute-done | bytes 4194336 | tf_op jit(solution)/shard_map/ppermute | solution.py:14
  452.7 5.8 collective-permute-done.1
  458.4 4.2 slice_select_fusion.1
  462.6 2.0 copy-done.2
  465.8 7.6 %fusion.3 = f32[256,256]{1,0:T(8,128)} fusion(f32[8192,128]{0,1:T(8,128)S(1)} %get-tuple-element.78, f32[8192,128]{0,1:T(8,128)S(1)} %get-tuple-element.77), kind=kOutput, calls=%fused_computation.13 | convolution fusion | flops 6444548096 | bytes 8650752 | tf_op jit(solution)/shard_map/dot_general | solution.py:36
  473.4 41.7 %all-reduce.6.cloned.1.call-done = f32[256,256]{1,0:T(8,128)} async-done(((f32[256,256]{1,0:T(8,128)}), f32[256,256]{1,0:T(8,128)}) %all-reduce.6.cloned.1.call-update) | async-done | bytes 262160 | tf_op jit(solution)/shard_map/psum | solution.py:46
  517.2 11.9 %cholesky.282 = f32[128,128]{1,0:T(8,128)S(1)} custom-call(f32[128,128]{1,0:T(8,128)S(1)} %cholesky.352), custom_call_target="Cholesky" | custom-call | tf_op jit(solution)/shard_map/jit(cholesky)/cholesky | solution.py:30
  529.1 9.8 %custom-call.21 = f32[1,128,128]{1,2,0:T(8,128)S(1)} custom-call(f32[1,128,128]{2,1,0:T(8,128)S(1)} %get-tuple-element.88), custom_call_target="InvertDiagBlocksLowerTriangular" | custom-call | tf_op jit(solution)/shard_map/jit(cholesky)/cholesky | solution.py:30
  539.4 11.7 %cholesky.299 = f32[128,128]{1,0:T(8,128)S(1)} custom-call(f32[128,128]{1,0:T(8,128)S(1)} %convolution_subtract_fusion.5), custom_call_target="Cholesky" | custom-call | tf_op jit(solution)/shard_map/jit(cholesky)/cholesky | solution.py:30
  553.7 3.8 while.10
  557.5 19.9 %custom-call.22 = f32[2,128,128]{1,2,0:T(8,128)S(1)} custom-call(f32[2,128,128]{2,1,0:T(8,128)S(1)} %get-tuple-element.35), custom_call_target="InvertDiagBlocksLowerTriangular" | custom-call | tf_op jit(solution)/shard_map/triangular_solve/custom-call.0 | solution.py:31
  578.4 1.4 fusion.15
  580.6 11.7 %cholesky.316 = f32[128,128]{1,0:T(8,128)S(1)} custom-call(f32[128,128]{1,0:T(8,128)S(1)} %cholesky.355), custom_call_target="Cholesky" | custom-call | tf_op jit(solution)/shard_map/jit(cholesky)/cholesky | solution.py:30
  592.4 9.8 %custom-call.23 = f32[1,128,128]{1,2,0:T(8,128)S(1)} custom-call(f32[1,128,128]{2,1,0:T(8,128)S(1)} %get-tuple-element.84), custom_call_target="InvertDiagBlocksLowerTriangular" | custom-call | tf_op jit(solution)/shard_map/jit(cholesky)/cholesky | solution.py:30
  602.7 11.7 %cholesky.333 = f32[128,128]{1,0:T(8,128)S(1)} custom-call(f32[128,128]{1,0:T(8,128)S(1)} %convolution_subtract_fusion.4), custom_call_target="Cholesky" | custom-call | tf_op jit(solution)/shard_map/jit(cholesky)/cholesky | solution.py:30
  617.0 4.1 while.11
  621.1 19.7 %custom-call.24 = f32[2,128,128]{1,2,0:T(8,128)S(1)} custom-call(f32[2,128,128]{2,1,0:T(8,128)S(1)} %get-tuple-element.36), custom_call_target="InvertDiagBlocksLowerTriangular" | custom-call | tf_op jit(solution)/shard_map/triangular_solve/custom-call.0 | solution.py:31
  641.8 17.7 %fusion.2 = f32[8192,256]{1,0:T(8,128)} fusion(f32[8192,128]{0,1:T(8,128)} %copy-done.3, f32[8192,128]{0,1:T(8,128)} %copy-done.2, f32[128,256]{1,0:T(8,128)S(1)} %fusion.37, f32[128,256]{1,0:T(8,128)S(1)} %fusion.28), kind=kOutput, calls=%fused_computation.12 | convolution fusion | flops 6444613632 | bytes 17039360 | tf_op jit(solution)/shard_map/dot_general | solution.py:88
  (102 shorter events, 29.7 us)
Async XLA Ops:
  6.5 209.8 %all-reduce.4.cloned.1.call-start = ((), (), s32[]{:S(2)}) async-start(), calls=%async_computation.1 | async-start | bytes 524288 | tf_op jit(solution)/shard_map/psum | solution.py:46
  162.9 3.4 copy-start
  181.3 333.8 %all-reduce.6.cloned.1.call-start = ((), (), s32[]{:S(2)}) async-start(), calls=%async_computation.2 | async-start | bytes 524288 | tf_op jit(solution)/shard_map/psum | solution.py:46
  353.6 5.9 copy-start.1
  359.5 93.2 %collective-permute-start = (f32[8192,128]{0,1:T(8,128)}, f32[8192,128]{0,1:T(8,128)}, u32[]{:S(2)}, u32[]{:S(2)}) collective-permute-start(f32[8192,128]{0,1:T(8,128)} %get-tuple-element.79), channel_id=1, source_target_pairs={{0,4},{4,8},{8,12},{12,16},{16,20},{20,24},{24,28},{28,32},{32,36}... | collective-permute-start | bytes 12582920 | tf_op jit(solution)/shard_map/ppermute | solution.py:14
  364.5 93.9 %collective-permute-start.1 = (f32[8192,128]{0,1:T(8,128)}, f32[8192,128]{0,1:T(8,128)}, u32[]{:S(2)}, u32[]{:S(2)}) collective-permute-start(f32[8192,128]{0,1:T(8,128)} %get-tuple-element.80), channel_id=1, source_target_pairs={{4,0},{8,4},{12,8},{16,12},{20,16},{24,20},{28,24},{32,28},{36,32}... | collective-permute-start | bytes 12582920 | tf_op jit(solution)/shard_map/ppermute | solution.py:14
  462.6 2.0 copy-start.2
  462.6 3.2 copy-start.3
Sparse Core Ops, SparseCore 0:
  181.4 34.8 all-reduce.3
  473.5 41.5 all-reduce.5
where the time goes:
time: 671 us; the launch traced here: 667 us
  other arithmetic  231 us (34%)
  waiting for transfers between devices  169 us (25%)
  blocking collectives  107 us (16%)
  local copies, waits for them, and re-layouts  68.7 us (10%)
  matrix products  64.3 us (10%)
  between operations  19.2 us (3%)
  starting transfers between devices  6.8 us (1%)
    another operation x27, other arithmetic, pair_rotation(): factor = jnp.linalg.cholesky(normal_matrix)  138 us
    all_to_all x1, blocking collectives, local(): lax.all_to_all(ordered, 'col', split_axis=1, concat_axis=0, tiled=True)  107 us
    ppermute x2, waiting for transfers between devices, shifted(): lax.ppermute(value, axis, [(source, source + steps) for source in range(l...  92.2 us
    another operation x9, other arithmetic, pair_rotation(): lax.linalg.triangular_solve(factor, product.T, left_side=True, lower=True)  79 us
    psum x2, waiting for transfers between devices, row_total(): return lax.psum(partial_gram, 'row')  76.7 us
    gather x3, local copies, waits for them, and re-layouts, local(): jnp.take(blocks, pairing, axis=1).reshape(local_rows, col_count, pair_width)  25.8 us
    dot_general x2, matrix products, local_gram(): lax.dot_general(pair_rows, pair_rows, (((0,), (0,)), ((), ())), precision...  22.5 us
    dot_general x1, matrix products, local(): jnp.dot(pair_rows, rotation, precision=lax.Precision.HIGHEST, preferred_e...  17.7 us
  transfers between devices with their start and end apart: 4, of which 4 were waited for; matrix products, arithmetic and copies ran while one was open for 0% of the time, Pallas kernels for 0%

commit v1 on v0

--- a/solution.py
+++ b/solution.py
@@ -43,7 +43,7 @@
 
 
 def row_total(partial_gram):
-    return lax.psum(partial_gram, "row")
+    return jnp.sum(lax.all_gather(partial_gram, "row"), axis=0)
 
 
 def send_down(lower_half):

time: 671 us -> 639 us (0.952)
  waiting for transfers between devices: 169 us -> 138 us
    psum x2 -> x0, waiting for transfers between devices: 76.7 us -> none  [row_total(): return lax.psum(partial_gram, 'row')]
    all_gather x0 -> x2, waiting for transfers between devices: none -> 46 us  [row_total(): return jnp.sum(lax.all_gather(partial_gram, 'row'), axis=0)]
where the time goes in v1:
time: 639 us; the launch traced here: 635 us
  other arithmetic  234 us (37%)
  waiting for transfers between devices  138 us (22%)
  blocking collectives  107 us (17%)
  local copies, waits for them, and re-layouts  68.7 us (11%)
  matrix products  60.6 us (9%)
  between operations  19.2 us (3%)
  starting transfers between devices  6.8 us (1%)
    another operation x27, other arithmetic, pair_rotation(): factor = jnp.linalg.cholesky(normal_matrix)  138 us
    all_to_all x1, blocking collectives, local(): lax.all_to_all(ordered, 'col', split_axis=1, concat_axis=0, tiled=True)  107 us
    ppermute x2, waiting for transfers between devices, shifted(): lax.ppermute(value, axis, [(source, source + steps) for source in range(l...  92.1 us
    another operation x9, other arithmetic, pair_rotation(): lax.linalg.triangular_solve(factor, product.T, left_side=True, lower=True)  79 us
    all_gather x2, waiting for transfers between devices, row_total(): return jnp.sum(lax.all_gather(partial_gram, 'row'), axis=0)  46 us
    gather x3, local copies, waits for them, and re-layouts, local(): jnp.take(blocks, pairing, axis=1).reshape(local_rows, col_count, pair_width)  25.8 us
    dot_general x2, matrix products, local_gram(): lax.dot_general(pair_rows, pair_rows, (((0,), (0,)), ((), ())), precision...  22.5 us
    dot_general x1, matrix products, local(): jnp.dot(pair_rows, rotation, precision=lax.Precision.HIGHEST, preferred_e...  17.7 us
  transfers between devices with their start and end apart: 4, of which 4 were waited for; matrix products, arithmetic and copies ran while one was open for 0% of the time, Pallas kernels for 0%

profile of v1, /device:TPU:1, one launch (start us, length us, event | category | flops | bytes accessed | tf_op | source)
XLA Modules:
  0.0 634.7 jit_solution(18035039633187954420)
XLA Ops:
  7.9 9.0 %copy.17 = f32[256,8192]{0,1:T(8,128)} copy(f32[256,8192]{1,0:T(8,128)} %param.5) | data formatting | bytes 16777216 | tf_op args[0]
  16.8 9.0 %copy.18 = f32[256,64,128]{2,0,1:T(8,128)} copy(f32[256,64,128]{0,2,1:T(8,128)} %bitcast.169) | data formatting | bytes 16777216 | tf_op jit(solution)/shard_map/reshape | solution.py:75
  25.8 7.9 %gather_fusion = f32[64,256,128]{2,1,0:T(8,128)} fusion(f32[256,64,128]{2,0,1:T(8,128)} %copy.18, s32[1024]{0:T(1024)S(1)} %pad_clamp_fusion), kind=kCustom, calls=%fused_computation | custom fusion | bytes 16777472 | tf_op jit(solution)/shard_map/jit(_take)/gather | solution.py:76
  33.7 9.0 %copy.19 = f32[256,64,128]{0,2,1:T(8,128)} copy(f32[256,64,128]{2,0,1:T(8,128)} %bitcast.167) | data formatting | bytes 16777216 | tf_op jit(solution)/shard_map/jit(_take)/gather | solution.py:76
  42.7 8.9 %copy.20 = f32[256,32,256]{2,0,1:T(8,128)} copy(f32[256,32,256]{0,2,1:T(8,128)} %bitcast.168) | data formatting | bytes 16777216 | tf_op jit(solution)/shard_map/jit(_take)/gather | solution.py:76
  51.9 4.3 broadcast_select_fusion
  56.2 106.7 %all_to_all.15 = f32[256,32,256]{2,0,1:T(8,128)S(1)} all-to-all(f32[256,32,256]{2,0,1:T(8,128)S(1)} %broadcast_select_fusion), channel_id=1, replica_groups=mesh['col'=32,'row'=4] {'col'}, dimensions={1} | all-to-all | bytes 16777216 | tf_op jit(solution)/shard_map/all_to_all | solution.py:77
  162.9 3.4 copy-done
  166.3 15.0 %fusion.4 = f32[256,256]{1,0:T(8,128)} fusion(f32[256,32,256]{2,0,1:T(8,128)S(1)} %all_to_all.15), kind=kOutput, calls=%fused_computation.18 | convolution fusion | flops 6442450944 | bytes 8650752 | tf_op jit(solution)/shard_map/dot_general | solution.py:36
  181.4 19.6 %all-gather.5.cloned.1.call-done = f32[1024,256]{1,0:T(8,128)} async-done(((f32[256,256]{1,0:T(8,128)}), f32[1024,256]{1,0:T(8,128)}) %all-gather.5.cloned.1.call-update) | async-done | bytes 1048592 | tf_op jit(solution)/shard_map/all_gather | solution.py:46
  200.9 1.3 reduce_sum.18
  203.3 11.7 %cholesky.214 = f32[128,128]{1,0:T(8,128)S(1)} custom-call(f32[128,128]{1,0:T(8,128)S(1)} %cholesky.346), custom_call_target="Cholesky" | custom-call | tf_op jit(solution)/shard_map/jit(cholesky)/cholesky | solution.py:30
  215.1 9.8 %custom-call.17 = f32[1,128,128]{1,2,0:T(8,128)S(1)} custom-call(f32[1,128,128]{2,1,0:T(8,128)S(1)} %get-tuple-element.96), custom_call_target="InvertDiagBlocksLowerTriangular" | custom-call | tf_op jit(solution)/shard_map/jit(cholesky)/cholesky | solution.py:30
  225.4 11.7 %cholesky.231 = f32[128,128]{1,0:T(8,128)S(1)} custom-call(f32[128,128]{1,0:T(8,128)S(1)} %convolution_subtract_fusion.7), custom_call_target="Cholesky" | custom-call | tf_op jit(solution)/shard_map/jit(cholesky)/cholesky | solution.py:30
  239.3 4.2 while.8
  240.1 1.3 bitcast_dynamic-update-slice_fusion.8
  242.2 1.3 bitcast_dynamic-update-slice_fusion.8
  243.5 19.7 %custom-call.18 = f32[2,128,128]{1,2,0:T(8,128)S(1)} custom-call(f32[2,128,128]{2,1,0:T(8,128)S(1)} %get-tuple-element.33), custom_call_target="InvertDiagBlocksLowerTriangular" | custom-call | tf_op jit(solution)/shard_map/triangular_solve/custom-call.0 | solution.py:31
  265.4 11.7 %cholesky.248 = f32[128,128]{1,0:T(8,128)S(1)} custom-call(f32[128,128]{1,0:T(8,128)S(1)} %cholesky.349), custom_call_target="Cholesky" | custom-call | tf_op jit(solution)/shard_map/jit(cholesky)/cholesky | solution.py:30
  277.2 9.8 %custom-call.19 = f32[1,128,128]{1,2,0:T(8,128)S(1)} custom-call(f32[1,128,128]{2,1,0:T(8,128)S(1)} %get-tuple-element.92), custom_call_target="InvertDiagBlocksLowerTriangular" | custom-call | tf_op jit(solution)/shard_map/jit(cholesky)/cholesky | solution.py:30
  287.5 11.7 %cholesky.265 = f32[128,128]{1,0:T(8,128)S(1)} custom-call(f32[128,128]{1,0:T(8,128)S(1)} %convolution_subtract_fusion.6), custom_call_target="Cholesky" | custom-call | tf_op jit(solution)/shard_map/jit(cholesky)/cholesky | solution.py:30
  301.9 4.3 while.9
  302.8 1.3 bitcast_dynamic-update-slice_fusion.9
  304.9 1.3 bitcast_dynamic-update-slice_fusion.9
  306.2 19.7 %custom-call.20 = f32[2,128,128]{1,2,0:T(8,128)S(1)} custom-call(f32[2,128,128]{2,1,0:T(8,128)S(1)} %get-tuple-element.34), custom_call_target="InvertDiagBlocksLowerTriangular" | custom-call | tf_op jit(solution)/shard_map/triangular_solve/custom-call.0 | solution.py:31
  326.9 10.7 %fusion.11 = f32[8192,256]{0,1:T(8,128)S(1)} fusion(f32[8192,256]{1,0:T(8,128)} %bitcast.166, f32[128,256]{1,0:T(8,128)S(1)} %fusion.45, f32[128,256]{1,0:T(8,128)S(1)} %fusion.32), kind=kOutput, calls=%fused_computation.35 | convolution fusion | flops 6442516480 | bytes 17039360 | tf_op jit(solution)/shard_map/dot_general | solution.py:58
  337.6 4.1 slice_select_fusion.2
  341.8 1.8 copy-done.1
  343.6 5.1 collective-permute-start
  348.6 1.7 collective-permute-start.1
  350.3 86.3 %collective-permute-done = f32[8192,128]{0,1:T(8,128)} collective-permute-done((f32[8192,128]{0,1:T(8,128)}, f32[8192,128]{0,1:T(8,128)}, u32[]{:S(2)}, u32[]{:S(2)}) %collective-permute-start) | collective-permute-done | bytes 4194336 | tf_op jit(solution)/shard_map/ppermute | solution.py:14
  436.7 5.8 collective-permute-done.1
  442.4 4.2 slice_select_fusion.1
  446.6 2.0 copy-done.2
  449.8 7.6 %fusion.3 = f32[256,256]{1,0:T(8,128)} fusion(f32[8192,128]{0,1:T(8,128)S(1)} %get-tuple-element.78, f32[8192,128]{0,1:T(8,128)S(1)} %get-tuple-element.77), kind=kOutput, calls=%fused_computation.13 | convolution fusion | flops 6444548096 | bytes 8650752 | tf_op jit(solution)/shard_map/dot_general | solution.py:36
  457.4 26.5 %all-gather.7.cloned.1.call-done = f32[1024,256]{1,0:T(8,128)} async-done(((f32[256,256]{1,0:T(8,128)}), f32[1024,256]{1,0:T(8,128)}) %all-gather.7.cloned.1.call-update) | async-done | bytes 1048592 | tf_op jit(solution)/shard_map/all_gather | solution.py:46
  483.9 1.3 reduce_sum.19
  486.3 11.9 %cholesky.282 = f32[128,128]{1,0:T(8,128)S(1)} custom-call(f32[128,128]{1,0:T(8,128)S(1)} %cholesky.352), custom_call_target="Cholesky" | custom-call | tf_op jit(solution)/shard_map/jit(cholesky)/cholesky | solution.py:30
  498.2 9.8 %custom-call.21 = f32[1,128,128]{1,2,0:T(8,128)S(1)} custom-call(f32[1,128,128]{2,1,0:T(8,128)S(1)} %get-tuple-element.88), custom_call_target="InvertDiagBlocksLowerTriangular" | custom-call | tf_op jit(solution)/shard_map/jit(cholesky)/cholesky | solution.py:30
  508.5 11.7 %cholesky.299 = f32[128,128]{1,0:T(8,128)S(1)} custom-call(f32[128,128]{1,0:T(8,128)S(1)} %convolution_subtract_fusion.5), custom_call_target="Cholesky" | custom-call | tf_op jit(solution)/shard_map/jit(cholesky)/cholesky | solution.py:30
  522.7 3.8 while.10
  526.6 19.9 %custom-call.22 = f32[2,128,128]{1,2,0:T(8,128)S(1)} custom-call(f32[2,128,128]{2,1,0:T(8,128)S(1)} %get-tuple-element.35), custom_call_target="InvertDiagBlocksLowerTriangular" | custom-call | tf_op jit(solution)/shard_map/triangular_solve/custom-call.0 | solution.py:31
  548.8 11.7 %cholesky.316 = f32[128,128]{1,0:T(8,128)S(1)} custom-call(f32[128,128]{1,0:T(8,128)S(1)} %cholesky.355), custom_call_target="Cholesky" | custom-call | tf_op jit(solution)/shard_map/jit(cholesky)/cholesky | solution.py:30
  560.5 9.8 %custom-call.23 = f32[1,128,128]{1,2,0:T(8,128)S(1)} custom-call(f32[1,128,128]{2,1,0:T(8,128)S(1)} %get-tuple-element.84), custom_call_target="InvertDiagBlocksLowerTriangular" | custom-call | tf_op jit(solution)/shard_map/jit(cholesky)/cholesky | solution.py:30
  570.8 11.7 %cholesky.333 = f32[128,128]{1,0:T(8,128)S(1)} custom-call(f32[128,128]{1,0:T(8,128)S(1)} %convolution_subtract_fusion.4), custom_call_target="Cholesky" | custom-call | tf_op jit(solution)/shard_map/jit(cholesky)/cholesky | solution.py:30
  585.1 4.1 while.11
  589.2 19.7 %custom-call.24 = f32[2,128,128]{1,2,0:T(8,128)S(1)} custom-call(f32[2,128,128]{2,1,0:T(8,128)S(1)} %get-tuple-element.36), custom_call_target="InvertDiagBlocksLowerTriangular" | custom-call | tf_op jit(solution)/shard_map/triangular_solve/custom-call.0 | solution.py:31
  609.9 17.7 %fusion.2 = f32[8192,256]{1,0:T(8,128)} fusion(f32[8192,128]{0,1:T(8,128)} %copy-done.3, f32[8192,128]{0,1:T(8,128)} %copy-done.2, f32[128,256]{1,0:T(8,128)S(1)} %fusion.37, f32[128,256]{1,0:T(8,128)S(1)} %fusion.28), kind=kOutput, calls=%fused_computation.12 | convolution fusion | flops 6444613632 | bytes 17039360 | tf_op jit(solution)/shard_map/dot_general | solution.py:88
  (104 shorter events, 28.6 us)
Async XLA Ops:
  6.5 194.4 %all-gather.5.cloned.1.call-start = ((), (), s32[]{:S(2)}) async-start(), calls=%async_computation.1 | async-start | bytes 1310720 | tf_op jit(solution)/shard_map/all_gather | solution.py:46
  162.9 3.4 copy-start
  181.3 302.5 %all-gather.7.cloned.1.call-start = ((), (), s32[]{:S(2)}) async-start(), calls=%async_computation.2 | async-start | bytes 1310720 | tf_op jit(solution)/shard_map/all_gather | solution.py:46
  337.6 5.9 copy-start.1
  343.6 93.1 %collective-permute-start = (f32[8192,128]{0,1:T(8,128)}, f32[8192,128]{0,1:T(8,128)}, u32[]{:S(2)}, u32[]{:S(2)}) collective-permute-start(f32[8192,128]{0,1:T(8,128)} %get-tuple-element.79), channel_id=1, source_target_pairs={{0,4},{4,8},{8,12},{12,16},{16,20},{20,24},{24,28},{28,32},{32,36}... | collective-permute-start | bytes 12582920 | tf_op jit(solution)/shard_map/ppermute | solution.py:14
  348.6 93.8 %collective-permute-start.1 = (f32[8192,128]{0,1:T(8,128)}, f32[8192,128]{0,1:T(8,128)}, u32[]{:S(2)}, u32[]{:S(2)}) collective-permute-start(f32[8192,128]{0,1:T(8,128)} %get-tuple-element.80), channel_id=1, source_target_pairs={{4,0},{8,4},{12,8},{16,12},{20,16},{24,20},{28,24},{32,28},{36,32}... | collective-permute-start | bytes 12582920 | tf_op jit(solution)/shard_map/ppermute | solution.py:14
  446.6 2.0 copy-start.2
  446.6 3.2 copy-start.3
Sparse Core Ops, SparseCore 0:
  181.4 19.4 all-gather.4
  457.5 26.3 all-gather.6
